TPU v7x, 256 devices: a whole 4x4x8 slice. The times are simulated.
256 devices in a mesh: segment: 8 (over y, z_lo), frame: 32 (over x, z_hi, core).
Axes of the slice: x: 4, y: 4, z: 8 (z_hi: 4, z_lo: 2; z = z_hi * 2 + z_lo), core: 2. Of those that a mesh axis runs over, the one named last changes fastest.
Arguments:
- noisy_clips: bfloat16 [4, 32, 16, 16, 512], P(None, 'frame'), may hold values from -6 to 6
- conv_first: bfloat16 [8, 9, 512, 512], P('segment', None, 'frame'), may hold values from -0.09375 to 0.09375
- conv_second: bfloat16 [8, 9, 512, 512], P('segment', None, 'frame'), may hold values from -0.09375 to 0.09375
- temporal: bfloat16 [8, 3, 512, 512], P('segment', None, 'frame'), may hold values from -0.15625 to 0.15625
Outputs:
- denoised: bfloat16 [4, 32, 16, 16, 512], P(None, 'frame', 'segment')
All inputs are finite; a program needn't handle non-finite values.
Results may differ from a plain program's by a relative error of at most 0.013.
Values may be sent and summed in bfloat16 or wider, within the bound.
No kernel may reach another device: no remote copies, remote signals or barrier semaphores. Data moves between devices by JAX's collectives and lax.ppermute only.
A program may use at most 64 MiB of HBM per device.

v0:
```python
import jax
import jax.numpy as jnp
from jax import lax
from jax.sharding import PartitionSpec as P

skip_scale = 0.7071067811865476


def passed_along(shard, axis, by):
    length = lax.axis_size(axis)
    pairs = [(i, i + by) for i in range(length) if 0 <= i + by < length]
    return lax.ppermute(shard, axis, pairs)


def partner(shard, axis, bit):
    return lax.ppermute(shard, axis, [(i, i ^ 1 << bit) for i in range(lax.axis_size(axis))])


def extended_2(cells, sides, width):
    for axis, dim in sides:
        count = lax.axis_size(axis)
        ends = count - 1
        head = lax.slice_in_dim(cells, 0, width, axis=dim)
        tail = lax.slice_in_dim(cells, cells.shape[dim] - width, cells.shape[dim], axis=dim)
        cells = jnp.concatenate(
            [
                lax.ppermute(tail, axis, [(i, (i + 1) % count) for i in range(ends)]),
                cells,
                lax.ppermute(head, axis, [((i + 1) % count, i) for i in range(ends)]),
            ],
            axis=dim,
        )
    return cells


def broadcast(shard, axis, root):
    mine = lax.axis_index(axis) == root
    return lax.psum(jnp.where(mine, shard, jnp.zeros_like(shard)), axis)


def spatial(field_in, kernel):
    extent = field_in.shape[1]
    channels = field_in.shape[3]
    padded = jnp.pad(field_in, ((0, 0), (1, 1), (1, 1), (0, 0)))
    accumulated = jnp.zeros((field_in.shape[0] * extent * extent, channels), jnp.float32)
    for row_shift in range(3):
        for col_shift in range(3):
            window = padded[
                :, row_shift : row_shift + extent, col_shift : col_shift + extent, :
            ].reshape(-1, channels)
            accumulated = accumulated + jnp.dot(
                window, kernel[3 * row_shift + col_shift], preferred_element_type=jnp.float32
            )
    return accumulated.reshape(field_in.shape)


def temporal_mix(extended, kernel, frame_local):
    channels = extended.shape[3]
    out_shape = (frame_local,) + extended.shape[1:]
    accumulated = jnp.zeros(out_shape, jnp.float32)
    for offset in range(3):
        window = extended[offset : offset + frame_local].reshape(-1, channels)
        accumulated = accumulated + jnp.dot(
            window, kernel[offset], preferred_element_type=jnp.float32
        ).reshape(out_shape)
    return accumulated


def on_device(noisy_clips, conv_first, conv_second, temporal):
    sections = lax.axis_size("segment")
    segment_id = lax.axis_index("segment")
    first_full, second_full, time_full = (
        lax.all_gather(conv_first, "frame", axis=2, tiled=True),
        lax.all_gather(conv_second, "frame", axis=2, tiled=True),
        lax.all_gather(temporal, "frame", axis=2, tiled=True),
    )
    first_kernel = first_full[0]
    second_kernel = second_full[0]
    time_kernel = time_full[0]
    clip_count = noisy_clips.shape[0]
    frame_local = noisy_clips.shape[1]
    side_len = noisy_clips.shape[2]
    block_shape = noisy_clips.shape[1:]
    tick_count = clip_count + sections - 1
    half_sections = sections // 2
    is_up = segment_id >= half_sections
    side_store = jnp.zeros((clip_count,) + block_shape, jnp.bfloat16)
    out_store = jnp.zeros(noisy_clips.shape, jnp.bfloat16)
    prev_out = jnp.zeros(block_shape, jnp.bfloat16)

    def tick_step(carry, tick_index):
        prev_out, side_store, out_store = carry
        clip_now = tick_index - segment_id
        active = (clip_now >= 0) & (clip_now < clip_count)
        clip_slot = jnp.clip(clip_now, 0, clip_count - 1)
        own_input = lax.dynamic_index_in_dim(noisy_clips, clip_slot, 0, keepdims=False)
        received = passed_along(prev_out, "segment", 1)
        entering = jnp.where(segment_id == 0, own_input, received)
        mirrored = entering
        for bit_number in range(sections.bit_length() - 1):
            mirrored = partner(mirrored, "segment", bit_number)
        mirror_clip = tick_index - (sections - 1 - segment_id)
        written = (jnp.arange(clip_count) == mirror_clip) & is_up
        side_store = jnp.where(written[:, None, None, None, None], mirrored[None], side_store)
        skip_feature = lax.dynamic_index_in_dim(side_store, clip_slot, 0, keepdims=False)
        joined = (
            (entering.astype(jnp.float32) + skip_feature.astype(jnp.float32)) * skip_scale
        ).astype(jnp.bfloat16)
        section_in = jnp.where(is_up, joined, entering)
        activated = lax.cond(
            active,
            lambda: jax.nn.silu(spatial(section_in, first_kernel)).astype(jnp.bfloat16),
            lambda: jnp.zeros(block_shape, jnp.bfloat16),
        )
        extended = extended_2(activated, (("frame", 0),), 1)

        def second_pass():
            branch_sum = spatial(activated, second_kernel) + temporal_mix(
                extended, time_kernel, frame_local
            )
            return (section_in.astype(jnp.float32) + jax.nn.silu(branch_sum)).astype(jnp.bfloat16)

        section_out = lax.cond(active, second_pass, lambda: jnp.zeros(block_shape, jnp.bfloat16))
        finished = (jnp.arange(clip_count) == clip_slot) & active & (segment_id == sections - 1)
        out_store = jnp.where(finished[:, None, None, None, None], section_out[None], out_store)
        return ((section_out, side_store, out_store), None)

    final_carry, unused = lax.scan(
        tick_step, (prev_out, side_store, out_store), jnp.arange(tick_count, dtype=jnp.int32)
    )
    delivered = broadcast(final_carry[2], "segment", sections - 1)
    slab_rows = side_len // sections
    return lax.dynamic_slice_in_dim(delivered, segment_id * slab_rows, slab_rows, 2)


def solution(mesh):
    in_specs = (
        P(None, "frame", None, None, None),
        P("segment", None, "frame", None),
        P("segment", None, "frame", None),
        P("segment", None, "frame", None),
    )
    out_specs = P(None, "frame", "segment", None, None)
    return jax.shard_map(
        on_device, mesh=mesh, in_specs=in_specs, out_specs=out_specs, check_vma=False
    )
```

profile of v0, /device:TPU:2, one launch (start us, length us, event | category | flops | bytes accessed | tf_op | source)
XLA Modules:
  0.0 975.8 jit_solution(13421447813197799213)
XLA Ops:
  8.8 56.3 %all-gather.8.cloned.1.call-done = bf16[1,3,512,512]{3,2,1,0:T(8,128)(2,1)} async-done(((bf16[1,3,16,512]{3,2,1,0:T(8,128)(2,1)}), bf16[1,3,512,512]{3,2,1,0:T(8,128)(2,1)}) %all-gather.8.cloned.1.call-update) | async-done | bytes 1572880 | tf_op jit(solution)/shard_map/all_gather | solution.py:75
  65.1 63.4 %all-gather.4.cloned.1.call-done = bf16[1,9,512,512]{3,2,1,0:T(8,128)(2,1)} async-done(((bf16[1,9,16,512]{3,2,1,0:T(8,128)(2,1)}), bf16[1,9,512,512]{3,2,1,0:T(8,128)(2,1)}) %all-gather.4.cloned.1.call-update) | async-done | bytes 4718608 | tf_op jit(solution)/shard_map/all_gather | solution.py:73
  128.4 63.1 %all-gather.6.cloned.1.call-done = bf16[1,9,512,512]{3,2,1,0:T(8,128)(2,1)} async-done(((bf16[1,9,16,512]{3,2,1,0:T(8,128)(2,1)}), bf16[1,9,512,512]{3,2,1,0:T(8,128)(2,1)}) %all-gather.6.cloned.1.call-update) | async-done | bytes 4718608 | tf_op jit(solution)/shard_map/all_gather | solution.py:74
  192.3 682.3 %while.16 = (s32[]{:T(128)}, bf16[1,16,16,512]{3,2,1,0:T(8,128)(2,1)}, bf16[4,1,16,16,512]{4,3,2,1,0:T(8,128)(2,1)S(1)}, bf16[4,1,16,16,512]{4,3,2,1,0:T(8,128)(...) while((s32[]{:T(128)}, ...), condition=%wide.region_5.6_spmd.clone, body=%wide.region_0.5_spmd.clone.sunk | while | flops 2825650176 | bytes 99615424 | solution.py:128
  234.9 6.7 collective-permute-start.5
  245.5 7.0 conditional.7
  270.5 7.6 collective-permute-done.2
  278.8 7.2 collective-permute-done.3
  293.9 6.7 collective-permute-start.5
  307.3 7.0 conditional.7
  342.1 7.3 collective-permute-done.3
  357.3 6.7 collective-permute-start.5
  370.6 7.0 conditional.7
  397.8 7.7 collective-permute-done.2
  406.1 7.2 collective-permute-done.3
  421.2 6.7 collective-permute-start.5
  434.5 7.0 conditional.7
  468.4 7.5 collective-permute-done.3
  478.5 6.7 collective-permute-start.5
  491.1 14.6 %collective-permute-start = (bf16[1,16,16,512]{3,2,1,0:T(8,128)(2,1)}, bf16[1,16,16,512]{3,2,1,0:T(8,128)(2,1)S(1)}, u32[]{:S(2)}, u32[]{:S(2)}) collective-permute-start(bf16[1,16,16,512]{3,2,1,0:T(8,128)(2,1)} %get-tuple-element.343), channel_id=1, source_target_pairs={{0,32},{32,64},{64,96},{96,128},{128,160},{160,192},{192,224},{1,3... | collective-permute-start | bytes 786440 | tf_op jit(solution)/shard_map/while/body/eval_jaxpr/ppermute | solution.py:12
  510.8 6.9 collective-permute-start.1
  531.0 7.2 collective-permute-done.3
  562.9 15.2 %collective-permute-start.1 = (bf16[1,16,16,512]{3,2,1,0:T(8,128)(2,1)S(1)}, bf16[1,16,16,512]{3,2,1,0:T(8,128)(2,1)S(1)}, u32[]{:S(2)}, u32[]{:S(2)}) collective-permute-start(bf16[1,16,16,512]{3,2,1,0:T(8,128)(2,1)S(1)} %bitcast_select_fusion.2), channel_id=1, source_target_pairs={{0,32},{32,0},{64,96},{96,64},{128,160},{160,128},{192,224},{224,1... | collective-permute-start | bytes 786440 | tf_op jit(solution)/shard_map/while/body/eval_jaxpr/ppermute | solution.py:16
  594.0 7.3 collective-permute-done.3
  603.8 6.7 collective-permute-start.5
  637.9 11.0 %collective-permute-start.2 = (bf16[1,16,16,512]{3,2,1,0:T(8,128)(2,1)S(1)}, bf16[1,16,16,512]{3,2,1,0:T(8,128)(2,1)S(1)}, u32[]{:S(2)}, u32[]{:S(2)}) collective-permute-start(bf16[1,16,16,512]{3,2,1,0:T(8,128)(2,1)S(1)} %collective-permute-done.1), channel_id=1, source_target_pairs={{0,64},{32,96},{64,0},{96,32},{128,192},{160,224},{192,128},{224,1... | collective-permute-start | bytes 786440 | tf_op jit(solution)/shard_map/while/body/eval_jaxpr/ppermute | solution.py:16
  666.8 6.7 collective-permute-start.5
  699.2 13.0 %collective-permute-start.2 = (bf16[1,16,16,512]{3,2,1,0:T(8,128)(2,1)S(1)}, bf16[1,16,16,512]{3,2,1,0:T(8,128)(2,1)S(1)}, u32[]{:S(2)}, u32[]{:S(2)}) collective-permute-start(bf16[1,16,16,512]{3,2,1,0:T(8,128)(2,1)S(1)} %collective-permute-done.1), channel_id=1, source_target_pairs={{0,64},{32,96},{64,0},{96,32},{128,192},{160,224},{192,128},{224,1... | collective-permute-start | bytes 786440 | tf_op jit(solution)/shard_map/while/body/eval_jaxpr/ppermute | solution.py:16
  767.6 19.2 %collective-permute-start.3 = (bf16[1,16,16,512]{3,2,1,0:T(8,128)(2,1)S(1)}, bf16[1,16,16,512]{3,2,1,0:T(8,128)(2,1)S(1)}, u32[]{:S(2)}, u32[]{:S(2)}) collective-permute-start(bf16[1,16,16,512]{3,2,1,0:T(8,128)(2,1)S(1)} %collective-permute-done.2), channel_id=1, source_target_pairs={{0,128},{32,160},{64,192},{96,224},{128,0},{160,32},{192,64},{224,... | collective-permute-start | bytes 786440 | tf_op jit(solution)/shard_map/while/body/eval_jaxpr/ppermute | solution.py:16
  793.6 6.7 collective-permute-start.5
  835.9 15.5 %collective-permute-start.3 = (bf16[1,16,16,512]{3,2,1,0:T(8,128)(2,1)S(1)}, bf16[1,16,16,512]{3,2,1,0:T(8,128)(2,1)S(1)}, u32[]{:S(2)}, u32[]{:S(2)}) collective-permute-start(bf16[1,16,16,512]{3,2,1,0:T(8,128)(2,1)S(1)} %collective-permute-done.2), channel_id=1, source_target_pairs={{0,128},{32,160},{64,192},{96,224},{128,0},{160,32},{192,64},{224,... | collective-permute-start | bytes 786440 | tf_op jit(solution)/shard_map/while/body/eval_jaxpr/ppermute | solution.py:16
  875.7 92.0 %all-reduce.4.cloned.1.call-done = bf16[4,1,16,16,512]{4,3,2,1,0:T(8,128)(2,1)} async-done(((bf16[4,1,16,16,512]{4,3,2,1,0:T(8,128)(2,1)}), bf16[4,1,16,16,512]{4,3,2,1,0:T(8,128)(2,1)}) %all-reduce.4.cloned.1.call-update) | async-done | bytes 1048592 | tf_op jit(solution)/shard_map/psum | solution.py:38
  (352 shorter events, 490.3 us)
Async XLA Ops:
  6.5 58.5 %all-gather.8.cloned.1.call-start = ((), (), s32[]{:S(2)}) async-start(), calls=%async_computation.2 | async-start | bytes 1622016 | tf_op jit(solution)/shard_map/all_gather | solution.py:75
  7.3 121.2 %all-gather.4.cloned.1.call-start = ((), (), s32[]{:S(2)}) async-start(), calls=%async_computation | async-start | bytes 4866048 | tf_op jit(solution)/shard_map/all_gather | solution.py:73
  8.0 183.6 %all-gather.6.cloned.1.call-start = ((), (), s32[]{:S(2)}) async-start(), calls=%async_computation.1 | async-start | bytes 4866048 | tf_op jit(solution)/shard_map/all_gather | solution.py:74
  8.7 959.0 %all-reduce.4.cloned.1.call-start = ((), (), s32[]{:S(2)}) async-start(), calls=%async_computation.3 | async-start | bytes 2097152 | tf_op jit(solution)/shard_map/psum | solution.py:38
  233.0 10.7 %collective-permute-start.4 = (bf16[1,16,16,512]{3,2,1,0:T(8,128)(2,1)S(1)}, bf16[1,16,16,512]{3,2,1,0:T(8,128)(2,1)S(1)}, u32[]{:S(2)}, u32[]{:S(2)}) collective-permute-start(bf16[1,16,16,512]{3,2,1,0:T(8,128)(2,1)S(1)} %get-tuple-element.378), channel_id=1, source_target_pairs={{0,1},{1,2},{2,3},{3,4},{4,5},{5,6},{6,7},{7,8},{8,9},{9,10},{10,1... | collective-permute-start | bytes 786440 | tf_op jit(solution)/shard_map/while/body/eval_jaxpr/ppermute | solution.py:27
  292.0 10.9 %collective-permute-start.4 = (bf16[1,16,16,512]{3,2,1,0:T(8,128)(2,1)S(1)}, bf16[1,16,16,512]{3,2,1,0:T(8,128)(2,1)S(1)}, u32[]{:S(2)}, u32[]{:S(2)}) collective-permute-start(bf16[1,16,16,512]{3,2,1,0:T(8,128)(2,1)S(1)} %get-tuple-element.378), channel_id=1, source_target_pairs={{0,1},{1,2},{2,3},{3,4},{4,5},{5,6},{6,7},{7,8},{8,9},{9,10},{10,1... | collective-permute-start | bytes 786440 | tf_op jit(solution)/shard_map/while/body/eval_jaxpr/ppermute | solution.py:27
  293.9 13.4 %collective-permute-start.5 = (bf16[1,16,16,512]{3,2,1,0:T(8,128)(2,1)S(1)}, bf16[1,16,16,512]{3,2,1,0:T(8,128)(2,1)S(1)}, u32[]{:S(2)}, u32[]{:S(2)}) collective-permute-start(bf16[1,16,16,512]{3,2,1,0:T(8,128)(2,1)S(1)} %get-tuple-element.378), channel_id=1, source_target_pairs={{1,0},{2,1},{3,2},{4,3},{5,4},{6,5},{7,6},{8,7},{9,8},{10,9},{11,1... | collective-permute-start | bytes 786440 | tf_op jit(solution)/shard_map/while/body/eval_jaxpr/ppermute | solution.py:29
  355.3 10.8 %collective-permute-start.4 = (bf16[1,16,16,512]{3,2,1,0:T(8,128)(2,1)S(1)}, bf16[1,16,16,512]{3,2,1,0:T(8,128)(2,1)S(1)}, u32[]{:S(2)}, u32[]{:S(2)}) collective-permute-start(bf16[1,16,16,512]{3,2,1,0:T(8,128)(2,1)S(1)} %get-tuple-element.378), channel_id=1, source_target_pairs={{0,1},{1,2},{2,3},{3,4},{4,5},{5,6},{6,7},{7,8},{8,9},{9,10},{10,1... | collective-permute-start | bytes 786440 | tf_op jit(solution)/shard_map/while/body/eval_jaxpr/ppermute | solution.py:27
  357.3 13.4 %collective-permute-start.5 = (bf16[1,16,16,512]{3,2,1,0:T(8,128)(2,1)S(1)}, bf16[1,16,16,512]{3,2,1,0:T(8,128)(2,1)S(1)}, u32[]{:S(2)}, u32[]{:S(2)}) collective-permute-start(bf16[1,16,16,512]{3,2,1,0:T(8,128)(2,1)S(1)} %get-tuple-element.378), channel_id=1, source_target_pairs={{1,0},{2,1},{3,2},{4,3},{5,4},{6,5},{7,6},{8,7},{9,8},{10,9},{11,1... | collective-permute-start | bytes 786440 | tf_op jit(solution)/shard_map/while/body/eval_jaxpr/ppermute | solution.py:29
  419.2 10.8 %collective-permute-start.4 = (bf16[1,16,16,512]{3,2,1,0:T(8,128)(2,1)S(1)}, bf16[1,16,16,512]{3,2,1,0:T(8,128)(2,1)S(1)}, u32[]{:S(2)}, u32[]{:S(2)}) collective-permute-start(bf16[1,16,16,512]{3,2,1,0:T(8,128)(2,1)S(1)} %get-tuple-element.378), channel_id=1, source_target_pairs={{0,1},{1,2},{2,3},{3,4},{4,5},{5,6},{6,7},{7,8},{8,9},{9,10},{10,1... | collective-permute-start | bytes 786440 | tf_op jit(solution)/shard_map/while/body/eval_jaxpr/ppermute | solution.py:27
  421.2 13.3 %collective-permute-start.5 = (bf16[1,16,16,512]{3,2,1,0:T(8,128)(2,1)S(1)}, bf16[1,16,16,512]{3,2,1,0:T(8,128)(2,1)S(1)}, u32[]{:S(2)}, u32[]{:S(2)}) collective-permute-start(bf16[1,16,16,512]{3,2,1,0:T(8,128)(2,1)S(1)} %get-tuple-element.378), channel_id=1, source_target_pairs={{1,0},{2,1},{3,2},{4,3},{5,4},{6,5},{7,6},{8,7},{9,8},{10,9},{11,1... | collective-permute-start | bytes 786440 | tf_op jit(solution)/shard_map/while/body/eval_jaxpr/ppermute | solution.py:29
  476.5 10.7 %collective-permute-start.4 = (bf16[1,16,16,512]{3,2,1,0:T(8,128)(2,1)S(1)}, bf16[1,16,16,512]{3,2,1,0:T(8,128)(2,1)S(1)}, u32[]{:S(2)}, u32[]{:S(2)}) collective-permute-start(bf16[1,16,16,512]{3,2,1,0:T(8,128)(2,1)S(1)} %get-tuple-element.378), channel_id=1, source_target_pairs={{0,1},{1,2},{2,3},{3,4},{4,5},{5,6},{6,7},{7,8},{8,9},{9,10},{10,1... | collective-permute-start | bytes 786440 | tf_op jit(solution)/shard_map/while/body/eval_jaxpr/ppermute | solution.py:27
  491.1 18.7 %collective-permute-start = (bf16[1,16,16,512]{3,2,1,0:T(8,128)(2,1)}, bf16[1,16,16,512]{3,2,1,0:T(8,128)(2,1)S(1)}, u32[]{:S(2)}, u32[]{:S(2)}) collective-permute-start(bf16[1,16,16,512]{3,2,1,0:T(8,128)(2,1)} %get-tuple-element.343), channel_id=1, source_target_pairs={{0,32},{32,64},{64,96},{96,128},{128,160},{160,192},{192,224},{1,3... | collective-permute-start | bytes 786440 | tf_op jit(solution)/shard_map/while/body/eval_jaxpr/ppermute | solution.py:12
  510.8 11.3 %collective-permute-start.1 = (bf16[1,16,16,512]{3,2,1,0:T(8,128)(2,1)S(1)}, bf16[1,16,16,512]{3,2,1,0:T(8,128)(2,1)S(1)}, u32[]{:S(2)}, u32[]{:S(2)}) collective-permute-start(bf16[1,16,16,512]{3,2,1,0:T(8,128)(2,1)S(1)} %bitcast_select_fusion.2), channel_id=1, source_target_pairs={{0,32},{32,0},{64,96},{96,64},{128,160},{160,128},{192,224},{224,1... | collective-permute-start | bytes 786440 | tf_op jit(solution)/shard_map/while/body/eval_jaxpr/ppermute | solution.py:16
  538.7 10.8 %collective-permute-start.4 = (bf16[1,16,16,512]{3,2,1,0:T(8,128)(2,1)S(1)}, bf16[1,16,16,512]{3,2,1,0:T(8,128)(2,1)S(1)}, u32[]{:S(2)}, u32[]{:S(2)}) collective-permute-start(bf16[1,16,16,512]{3,2,1,0:T(8,128)(2,1)S(1)} %get-tuple-element.378), channel_id=1, source_target_pairs={{0,1},{1,2},{2,3},{3,4},{4,5},{5,6},{6,7},{7,8},{8,9},{9,10},{10,1... | collective-permute-start | bytes 786440 | tf_op jit(solution)/shard_map/while/body/eval_jaxpr/ppermute | solution.py:27
  540.6 13.0 %collective-permute-start.5 = (bf16[1,16,16,512]{3,2,1,0:T(8,128)(2,1)S(1)}, bf16[1,16,16,512]{3,2,1,0:T(8,128)(2,1)S(1)}, u32[]{:S(2)}, u32[]{:S(2)}) collective-permute-start(bf16[1,16,16,512]{3,2,1,0:T(8,128)(2,1)S(1)} %get-tuple-element.378), channel_id=1, source_target_pairs={{1,0},{2,1},{3,2},{4,3},{5,4},{6,5},{7,6},{8,7},{9,8},{10,9},{11,1... | collective-permute-start | bytes 786440 | tf_op jit(solution)/shard_map/while/body/eval_jaxpr/ppermute | solution.py:29
  562.9 21.5 %collective-permute-start.1 = (bf16[1,16,16,512]{3,2,1,0:T(8,128)(2,1)S(1)}, bf16[1,16,16,512]{3,2,1,0:T(8,128)(2,1)S(1)}, u32[]{:S(2)}, u32[]{:S(2)}) collective-permute-start(bf16[1,16,16,512]{3,2,1,0:T(8,128)(2,1)S(1)} %bitcast_select_fusion.2), channel_id=1, source_target_pairs={{0,32},{32,0},{64,96},{96,64},{128,160},{160,128},{192,224},{224,1... | collective-permute-start | bytes 786440 | tf_op jit(solution)/shard_map/while/body/eval_jaxpr/ppermute | solution.py:16
  601.8 10.8 %collective-permute-start.4 = (bf16[1,16,16,512]{3,2,1,0:T(8,128)(2,1)S(1)}, bf16[1,16,16,512]{3,2,1,0:T(8,128)(2,1)S(1)}, u32[]{:S(2)}, u32[]{:S(2)}) collective-permute-start(bf16[1,16,16,512]{3,2,1,0:T(8,128)(2,1)S(1)} %get-tuple-element.378), channel_id=1, source_target_pairs={{0,1},{1,2},{2,3},{3,4},{4,5},{5,6},{6,7},{7,8},{8,9},{9,10},{10,1... | collective-permute-start | bytes 786440 | tf_op jit(solution)/shard_map/while/body/eval_jaxpr/ppermute | solution.py:27
  603.8 12.2 %collective-permute-start.5 = (bf16[1,16,16,512]{3,2,1,0:T(8,128)(2,1)S(1)}, bf16[1,16,16,512]{3,2,1,0:T(8,128)(2,1)S(1)}, u32[]{:S(2)}, u32[]{:S(2)}) collective-permute-start(bf16[1,16,16,512]{3,2,1,0:T(8,128)(2,1)S(1)} %get-tuple-element.378), channel_id=1, source_target_pairs={{1,0},{2,1},{3,2},{4,3},{5,4},{6,5},{7,6},{8,7},{9,8},{10,9},{11,1... | collective-permute-start | bytes 786440 | tf_op jit(solution)/shard_map/while/body/eval_jaxpr/ppermute | solution.py:29
  637.9 16.8 %collective-permute-start.2 = (bf16[1,16,16,512]{3,2,1,0:T(8,128)(2,1)S(1)}, bf16[1,16,16,512]{3,2,1,0:T(8,128)(2,1)S(1)}, u32[]{:S(2)}, u32[]{:S(2)}) collective-permute-start(bf16[1,16,16,512]{3,2,1,0:T(8,128)(2,1)S(1)} %collective-permute-done.1), channel_id=1, source_target_pairs={{0,64},{32,96},{64,0},{96,32},{128,192},{160,224},{192,128},{224,1... | collective-permute-start | bytes 786440 | tf_op jit(solution)/shard_map/while/body/eval_jaxpr/ppermute | solution.py:16
  664.9 10.8 %collective-permute-start.4 = (bf16[1,16,16,512]{3,2,1,0:T(8,128)(2,1)S(1)}, bf16[1,16,16,512]{3,2,1,0:T(8,128)(2,1)S(1)}, u32[]{:S(2)}, u32[]{:S(2)}) collective-permute-start(bf16[1,16,16,512]{3,2,1,0:T(8,128)(2,1)S(1)} %get-tuple-element.378), channel_id=1, source_target_pairs={{0,1},{1,2},{2,3},{3,4},{4,5},{5,6},{6,7},{7,8},{8,9},{9,10},{10,1... | collective-permute-start | bytes 786440 | tf_op jit(solution)/shard_map/while/body/eval_jaxpr/ppermute | solution.py:27
  666.8 10.7 %collective-permute-start.5 = (bf16[1,16,16,512]{3,2,1,0:T(8,128)(2,1)S(1)}, bf16[1,16,16,512]{3,2,1,0:T(8,128)(2,1)S(1)}, u32[]{:S(2)}, u32[]{:S(2)}) collective-permute-start(bf16[1,16,16,512]{3,2,1,0:T(8,128)(2,1)S(1)} %get-tuple-element.378), channel_id=1, source_target_pairs={{1,0},{2,1},{3,2},{4,3},{5,4},{6,5},{7,6},{8,7},{9,8},{10,9},{11,1... | collective-permute-start | bytes 786440 | tf_op jit(solution)/shard_map/while/body/eval_jaxpr/ppermute | solution.py:29
  679.6 10.7 %collective-permute-start = (bf16[1,16,16,512]{3,2,1,0:T(8,128)(2,1)}, bf16[1,16,16,512]{3,2,1,0:T(8,128)(2,1)S(1)}, u32[]{:S(2)}, u32[]{:S(2)}) collective-permute-start(bf16[1,16,16,512]{3,2,1,0:T(8,128)(2,1)} %get-tuple-element.343), channel_id=1, source_target_pairs={{0,32},{32,64},{64,96},{96,128},{128,160},{160,192},{192,224},{1,3... | collective-permute-start | bytes 786440 | tf_op jit(solution)/shard_map/while/body/eval_jaxpr/ppermute | solution.py:12
  699.2 17.3 %collective-permute-start.2 = (bf16[1,16,16,512]{3,2,1,0:T(8,128)(2,1)S(1)}, bf16[1,16,16,512]{3,2,1,0:T(8,128)(2,1)S(1)}, u32[]{:S(2)}, u32[]{:S(2)}) collective-permute-start(bf16[1,16,16,512]{3,2,1,0:T(8,128)(2,1)S(1)} %collective-permute-done.1), channel_id=1, source_target_pairs={{0,64},{32,96},{64,0},{96,32},{128,192},{160,224},{192,128},{224,1... | collective-permute-start | bytes 786440 | tf_op jit(solution)/shard_map/while/body/eval_jaxpr/ppermute | solution.py:16
  727.6 10.8 %collective-permute-start.4 = (bf16[1,16,16,512]{3,2,1,0:T(8,128)(2,1)S(1)}, bf16[1,16,16,512]{3,2,1,0:T(8,128)(2,1)S(1)}, u32[]{:S(2)}, u32[]{:S(2)}) collective-permute-start(bf16[1,16,16,512]{3,2,1,0:T(8,128)(2,1)S(1)} %get-tuple-element.378), channel_id=1, source_target_pairs={{0,1},{1,2},{2,3},{3,4},{4,5},{5,6},{6,7},{7,8},{8,9},{9,10},{10,1... | collective-permute-start | bytes 786440 | tf_op jit(solution)/shard_map/while/body/eval_jaxpr/ppermute | solution.py:27
  729.6 13.1 %collective-permute-start.5 = (bf16[1,16,16,512]{3,2,1,0:T(8,128)(2,1)S(1)}, bf16[1,16,16,512]{3,2,1,0:T(8,128)(2,1)S(1)}, u32[]{:S(2)}, u32[]{:S(2)}) collective-permute-start(bf16[1,16,16,512]{3,2,1,0:T(8,128)(2,1)S(1)} %get-tuple-element.378), channel_id=1, source_target_pairs={{1,0},{2,1},{3,2},{4,3},{5,4},{6,5},{7,6},{8,7},{9,8},{10,9},{11,1... | collective-permute-start | bytes 786440 | tf_op jit(solution)/shard_map/while/body/eval_jaxpr/ppermute | solution.py:29
  767.6 23.5 %collective-permute-start.3 = (bf16[1,16,16,512]{3,2,1,0:T(8,128)(2,1)S(1)}, bf16[1,16,16,512]{3,2,1,0:T(8,128)(2,1)S(1)}, u32[]{:S(2)}, u32[]{:S(2)}) collective-permute-start(bf16[1,16,16,512]{3,2,1,0:T(8,128)(2,1)S(1)} %collective-permute-done.2), channel_id=1, source_target_pairs={{0,128},{32,160},{64,192},{96,224},{128,0},{160,32},{192,64},{224,... | collective-permute-start | bytes 786440 | tf_op jit(solution)/shard_map/while/body/eval_jaxpr/ppermute | solution.py:16
  791.7 10.8 %collective-permute-start.4 = (bf16[1,16,16,512]{3,2,1,0:T(8,128)(2,1)S(1)}, bf16[1,16,16,512]{3,2,1,0:T(8,128)(2,1)S(1)}, u32[]{:S(2)}, u32[]{:S(2)}) collective-permute-start(bf16[1,16,16,512]{3,2,1,0:T(8,128)(2,1)S(1)} %get-tuple-element.378), channel_id=1, source_target_pairs={{0,1},{1,2},{2,3},{3,4},{4,5},{5,6},{6,7},{7,8},{8,9},{9,10},{10,1... | collective-permute-start | bytes 786440 | tf_op jit(solution)/shard_map/while/body/eval_jaxpr/ppermute | solution.py:27
  793.6 13.3 %collective-permute-start.5 = (bf16[1,16,16,512]{3,2,1,0:T(8,128)(2,1)S(1)}, bf16[1,16,16,512]{3,2,1,0:T(8,128)(2,1)S(1)}, u32[]{:S(2)}, u32[]{:S(2)}) collective-permute-start(bf16[1,16,16,512]{3,2,1,0:T(8,128)(2,1)S(1)} %get-tuple-element.378), channel_id=1, source_target_pairs={{1,0},{2,1},{3,2},{4,3},{5,4},{6,5},{7,6},{8,7},{9,8},{10,9},{11,1... | collective-permute-start | bytes 786440 | tf_op jit(solution)/shard_map/while/body/eval_jaxpr/ppermute | solution.py:29
  835.9 20.8 %collective-permute-start.3 = (bf16[1,16,16,512]{3,2,1,0:T(8,128)(2,1)S(1)}, bf16[1,16,16,512]{3,2,1,0:T(8,128)(2,1)S(1)}, u32[]{:S(2)}, u32[]{:S(2)}) collective-permute-start(bf16[1,16,16,512]{3,2,1,0:T(8,128)(2,1)S(1)} %collective-permute-done.2), channel_id=1, source_target_pairs={{0,128},{32,160},{64,192},{96,224},{128,0},{160,32},{192,64},{224,... | collective-permute-start | bytes 786440 | tf_op jit(solution)/shard_map/while/body/eval_jaxpr/ppermute | solution.py:16
  857.3 10.8 %collective-permute-start.4 = (bf16[1,16,16,512]{3,2,1,0:T(8,128)(2,1)S(1)}, bf16[1,16,16,512]{3,2,1,0:T(8,128)(2,1)S(1)}, u32[]{:S(2)}, u32[]{:S(2)}) collective-permute-start(bf16[1,16,16,512]{3,2,1,0:T(8,128)(2,1)S(1)} %get-tuple-element.378), channel_id=1, source_target_pairs={{0,1},{1,2},{2,3},{3,4},{4,5},{5,6},{6,7},{7,8},{8,9},{9,10},{10,1... | collective-permute-start | bytes 786440 | tf_op jit(solution)/shard_map/while/body/eval_jaxpr/ppermute | solution.py:27
  859.2 13.3 %collective-permute-start.5 = (bf16[1,16,16,512]{3,2,1,0:T(8,128)(2,1)S(1)}, bf16[1,16,16,512]{3,2,1,0:T(8,128)(2,1)S(1)}, u32[]{:S(2)}, u32[]{:S(2)}) collective-permute-start(bf16[1,16,16,512]{3,2,1,0:T(8,128)(2,1)S(1)} %get-tuple-element.378), channel_id=1, source_target_pairs={{1,0},{2,1},{3,2},{4,3},{5,4},{6,5},{7,6},{8,7},{9,8},{10,9},{11,1... | collective-permute-start | bytes 786440 | tf_op jit(solution)/shard_map/while/body/eval_jaxpr/ppermute | solution.py:29
  (50 other events, 349.6 us)
Sparse Core Ops, SparseCore 0:
  10.0 55.0 all-gather.7
  67.7 60.6 all-gather.3
  131.1 60.4 all-gather.5
  875.8 91.8 all-reduce.3
where the time goes:
time: 978 us; the launch traced here: 976 us
  waiting for transfers between devices  577 us (59%)
  starting transfers between devices  273 us (28%)
  matrix products  46.2 us (5%)
  other arithmetic  32.5 us (3%)
  loops' own time  17.3 us (2%)
  local copies, waits for them, and re-layouts  17 us (2%)
  between operations  13.2 us (1%)
    ppermute x33, waiting for transfers between devices, partner(): lax.ppermute(shard, axis, [(i, i ^ 1 << bit) for i in range(lax.axis_size...  190 us
    ppermute x33, starting transfers between devices, partner(): lax.ppermute(shard, axis, [(i, i ^ 1 << bit) for i in range(lax.axis_size...  141 us
    psum x1, waiting for transfers between devices, broadcast(): return lax.psum(jnp.where(mine, shard, jnp.zeros_like(shard)), axis)  92 us
    ppermute x11, starting transfers between devices, extended_2(): lax.ppermute(head, axis, [((i + 1) % count, i) for i in range(ends)])  73.2 us
    all_gather x1, waiting for transfers between devices, on_device(): lax.all_gather(conv_first, 'frame', axis=2, tiled=True)  63.4 us
    all_gather x1, waiting for transfers between devices, on_device(): lax.all_gather(conv_second, 'frame', axis=2, tiled=True)  63.1 us
    all_gather x1, waiting for transfers between devices, on_device(): lax.all_gather(temporal, 'frame', axis=2, tiled=True)  56.3 us
    ppermute x11, waiting for transfers between devices, passed_along(): return lax.ppermute(shard, axis, pairs)  47.2 us
  transfers between devices with their start and end apart: 70, of which 70 were waited for; matrix products, arithmetic and copies ran while one was open for 1% of the time, Pallas kernels for 0%

commit v1 on v0

--- a/solution.py
+++ b/solution.py
@@ -69,9 +69,16 @@
 def on_device(noisy_clips, conv_first, conv_second, temporal):
     sections = lax.axis_size("segment")
     segment_id = lax.axis_index("segment")
+
+    def track_links(u):
+        next_value = lax.axis_size("frame")
+        u_next = jnp.stack([u] * next_value)
+        main = lax.all_to_all(u_next, "frame", 0, 0)
+        return jnp.concatenate(main, axis=2)
+
     first_full, second_full, time_full = (
         lax.all_gather(conv_first, "frame", axis=2, tiled=True),
-        lax.all_gather(conv_second, "frame", axis=2, tiled=True),
+        track_links(conv_second),
         lax.all_gather(temporal, "frame", axis=2, tiled=True),
     )
     first_kernel = first_full[0]

time: 978 us -> 955 us (0.976)
  waiting for transfers between devices: 577 us -> 539 us
    all_to_all x0 -> x1, waiting for transfers between devices: none -> 116 us  [track_links(): main = lax.all_to_all(u_next, 'frame', 0, 0)]
    all_gather x1 -> x0, waiting for transfers between devices: 63.1 us -> none  [on_device(): lax.all_gather(conv_second, 'frame', axis=2, tiled=True)]
    all_gather x1, waiting for transfers between devices: 56.3 us -> 0.01 us  [on_device(): lax.all_gather(temporal, 'frame', axis=2, tiled=True)]
    all_gather x1, waiting for transfers between devices: 63.4 us -> 30.2 us  [on_device(): lax.all_gather(conv_first, 'frame', axis=2, tiled=True)]
    all_to_all x0 -> x1, starting transfers between devices: none -> 11.7 us  [track_links(): main = lax.all_to_all(u_next, 'frame', 0, 0)]
  transfers between devices with their start and end apart: 70 -> 70, of which waited for: 70 -> 69; matrix products, arithmetic and copies ran while one was open for 1% -> 2% of each run, Pallas kernels for 0% -> 0%
where the time goes in v1:
time: 955 us; the launch traced here: 953 us
  waiting for transfers between devices  539 us (56%)
  starting transfers between devices  280 us (29%)
  matrix products  46.3 us (5%)
  other arithmetic  32.5 us (3%)
  local copies, waits for them, and re-layouts  25.3 us (3%)
  loops' own time  15.7 us (2%)
  between operations  13.2 us (1%)
    ppermute x33, waiting for transfers between devices, partner(): lax.ppermute(shard, axis, [(i, i ^ 1 << bit) for i in range(lax.axis_size...  182 us
    ppermute x33, starting transfers between devices, partner(): lax.ppermute(shard, axis, [(i, i ^ 1 << bit) for i in range(lax.axis_size...  146 us
    all_to_all x1, waiting for transfers between devices, track_links(): main = lax.all_to_all(u_next, 'frame', 0, 0)  116 us
    psum x1, waiting for transfers between devices, broadcast(): return lax.psum(jnp.where(mine, shard, jnp.zeros_like(shard)), axis)  95.3 us
    ppermute x11, starting transfers between devices, extended_2(): lax.ppermute(head, axis, [((i + 1) % count, i) for i in range(ends)])  73.2 us
    ppermute x11, waiting for transfers between devices, passed_along(): return lax.ppermute(shard, axis, pairs)  47.5 us
    ppermute x11, waiting for transfers between devices, extended_2(): lax.ppermute(head, axis, [((i + 1) % count, i) for i in range(ends)])  40.1 us
    dot_general x72, matrix products, spatial(): jnp.dot(window, kernel[3 * row_shift + col_shift], preferred_element_type...  39.3 us
  transfers between devices with their start and end apart: 70, of which 69 were waited for; matrix products, arithmetic and copies ran while one was open for 2% of the time, Pallas kernels for 0%

profile of v1, /device:TPU:2, one launch (start us, length us, event | category | flops | bytes accessed | tf_op | source)
XLA Modules:
  0.0 952.6 jit_solution(14303400762992597241)
XLA Ops:
  10.9 11.7 %all-to-all-start = ((bf16[32,1,9,16,512]{4,3,2,1,0:T(8,128)(2,1)}), bf16[32,1,9,16,512]{4,3,2,1,0:T(8,128)(2,1)}, u32[]{:S(2)}, u32[]{:S(2)}) async-start(bf16[32,1,9,16,512]{4,3,2,1,0:T(8,128)(2,1)} %stack.2), calls=%async_computation | async-start | bytes 9437184 | tf_op jit(solution)/shard_map/all_to_all | solution.py:76
  23.4 116.5 %all-to-all-done = bf16[32,1,9,16,512]{4,3,2,1,0:T(8,128)(2,1)} async-done(((bf16[32,1,9,16,512]{4,3,2,1,0:T(8,128)(2,1)}), bf16[32,1,9,16,512]{4,3,2,1,0:T(8,128)(2,1)}, u32[]{:S(2)}, u32[]{:S(2)}) %all-to-all-start) | async-done | bytes 4718624 | tf_op jit(solution)/shard_map/all_to_all | solution.py:76
  145.1 30.2 %all-gather.3.cloned.1.call-done = bf16[1,9,512,512]{3,2,1,0:T(8,128)(2,1)} async-done(((bf16[1,9,16,512]{3,2,1,0:T(8,128)(2,1)}), bf16[1,9,512,512]{3,2,1,0:T(8,128)(2,1)}) %all-gather.3.cloned.1.call-update) | async-done | bytes 4718608 | tf_op jit(solution)/shard_map/all_gather | solution.py:80
  176.1 672.0 %while.16 = (s32[]{:T(128)}, bf16[1,16,16,512]{3,2,1,0:T(8,128)(2,1)}, bf16[4,1,16,16,512]{4,3,2,1,0:T(8,128)(2,1)S(1)}, bf16[4,1,16,16,512]{4,3,2,1,0:T(8,128)(...) while((s32[]{:T(128)}, ...), condition=%wide.region_5.6_spmd.clone, body=%wide.region_0.5_spmd.clone.sunk | while | flops 2825650176 | bytes 99615424 | solution.py:135
  218.8 6.7 collective-permute-start.5
  229.3 7.0 conditional.7
  254.3 7.6 collective-permute-done.2
  262.6 7.2 collective-permute-done.3
  277.7 6.7 collective-permute-start.5
  291.1 7.0 conditional.7
  325.8 7.4 collective-permute-done.3
  341.1 6.7 collective-permute-start.5
  354.5 7.0 conditional.7
  381.6 7.7 collective-permute-done.2
  389.9 7.2 collective-permute-done.3
  405.1 6.7 collective-permute-start.5
  418.4 7.0 conditional.7
  451.6 7.4 collective-permute-done.3
  461.5 6.7 collective-permute-start.5
  474.1 14.5 %collective-permute-start = (bf16[1,16,16,512]{3,2,1,0:T(8,128)(2,1)}, bf16[1,16,16,512]{3,2,1,0:T(8,128)(2,1)S(1)}, u32[]{:S(2)}, u32[]{:S(2)}) collective-permute-start(bf16[1,16,16,512]{3,2,1,0:T(8,128)(2,1)} %get-tuple-element.343), channel_id=1, source_target_pairs={{0,32},{32,64},{64,96},{96,128},{128,160},{160,192},{192,224},{1,3... | collective-permute-start | bytes 786440 | tf_op jit(solution)/shard_map/while/body/eval_jaxpr/ppermute | solution.py:12
  493.8 7.5 collective-permute-start.1
  514.4 7.2 collective-permute-done.3
  524.2 6.7 collective-permute-start.5
  545.9 17.8 %collective-permute-start.1 = (bf16[1,16,16,512]{3,2,1,0:T(8,128)(2,1)S(1)}, bf16[1,16,16,512]{3,2,1,0:T(8,128)(2,1)S(1)}, u32[]{:S(2)}, u32[]{:S(2)}) collective-permute-start(bf16[1,16,16,512]{3,2,1,0:T(8,128)(2,1)S(1)} %bitcast_select_fusion.2), channel_id=1, source_target_pairs={{0,32},{32,0},{64,96},{96,64},{128,160},{160,128},{192,224},{224,1... | collective-permute-start | bytes 786440 | tf_op jit(solution)/shard_map/while/body/eval_jaxpr/ppermute | solution.py:16
  576.9 7.2 collective-permute-done.3
  617.7 11.0 %collective-permute-start.2 = (bf16[1,16,16,512]{3,2,1,0:T(8,128)(2,1)S(1)}, bf16[1,16,16,512]{3,2,1,0:T(8,128)(2,1)S(1)}, u32[]{:S(2)}, u32[]{:S(2)}) collective-permute-start(bf16[1,16,16,512]{3,2,1,0:T(8,128)(2,1)S(1)} %collective-permute-done.1), channel_id=1, source_target_pairs={{0,64},{32,96},{64,0},{96,32},{128,192},{160,224},{192,128},{224,1... | collective-permute-start | bytes 786440 | tf_op jit(solution)/shard_map/while/body/eval_jaxpr/ppermute | solution.py:16
  677.5 14.3 %collective-permute-start.2 = (bf16[1,16,16,512]{3,2,1,0:T(8,128)(2,1)S(1)}, bf16[1,16,16,512]{3,2,1,0:T(8,128)(2,1)S(1)}, u32[]{:S(2)}, u32[]{:S(2)}) collective-permute-start(bf16[1,16,16,512]{3,2,1,0:T(8,128)(2,1)S(1)} %collective-permute-done.1), channel_id=1, source_target_pairs={{0,64},{32,96},{64,0},{96,32},{128,192},{160,224},{192,128},{224,1... | collective-permute-start | bytes 786440 | tf_op jit(solution)/shard_map/while/body/eval_jaxpr/ppermute | solution.py:16
  691.8 6.9 collective-permute-done.2
  748.4 15.0 %collective-permute-start.3 = (bf16[1,16,16,512]{3,2,1,0:T(8,128)(2,1)S(1)}, bf16[1,16,16,512]{3,2,1,0:T(8,128)(2,1)S(1)}, u32[]{:S(2)}, u32[]{:S(2)}) collective-permute-start(bf16[1,16,16,512]{3,2,1,0:T(8,128)(2,1)S(1)} %collective-permute-done.2), channel_id=1, source_target_pairs={{0,128},{32,160},{64,192},{96,224},{128,0},{160,32},{192,64},{224,... | collective-permute-start | bytes 786440 | tf_op jit(solution)/shard_map/while/body/eval_jaxpr/ppermute | solution.py:16
  770.3 6.7 collective-permute-start.5
  807.4 18.8 %collective-permute-start.3 = (bf16[1,16,16,512]{3,2,1,0:T(8,128)(2,1)S(1)}, bf16[1,16,16,512]{3,2,1,0:T(8,128)(2,1)S(1)}, u32[]{:S(2)}, u32[]{:S(2)}) collective-permute-start(bf16[1,16,16,512]{3,2,1,0:T(8,128)(2,1)S(1)} %collective-permute-done.2), channel_id=1, source_target_pairs={{0,128},{32,160},{64,192},{96,224},{128,0},{160,32},{192,64},{224,... | collective-permute-start | bytes 786440 | tf_op jit(solution)/shard_map/while/body/eval_jaxpr/ppermute | solution.py:16
  849.2 95.3 %all-reduce.4.cloned.1.call-done = bf16[4,1,16,16,512]{4,3,2,1,0:T(8,128)(2,1)} async-done(((bf16[4,1,16,16,512]{4,3,2,1,0:T(8,128)(2,1)}), bf16[4,1,16,16,512]{4,3,2,1,0:T(8,128)(2,1)}) %all-reduce.4.cloned.1.call-update) | async-done | bytes 1048592 | tf_op jit(solution)/shard_map/psum | solution.py:38
  (353 shorter events, 486.0 us)
Async XLA Ops:
  6.5 138.6 %all-gather.5.cloned.1.call-start = ((), (), s32[]{:S(2)}) async-start(), calls=%async_computation.2 | async-start | bytes 1622016 | tf_op jit(solution)/shard_map/all_gather | solution.py:82
  10.9 129.0 %all-to-all-start = ((bf16[32,1,9,16,512]{4,3,2,1,0:T(8,128)(2,1)}), bf16[32,1,9,16,512]{4,3,2,1,0:T(8,128)(2,1)}, u32[]{:S(2)}, u32[]{:S(2)}) async-start(bf16[32,1,9,16,512]{4,3,2,1,0:T(8,128)(2,1)} %stack.2), calls=%async_computation | async-start | bytes 9437184 | tf_op jit(solution)/shard_map/all_to_all | solution.py:76
  22.6 152.8 %all-gather.3.cloned.1.call-start = ((), (), s32[]{:S(2)}) async-start(), calls=%async_computation.1 | async-start | bytes 4866048 | tf_op jit(solution)/shard_map/all_gather | solution.py:80
  23.4 921.2 %all-reduce.4.cloned.1.call-start = ((), (), s32[]{:S(2)}) async-start(), calls=%async_computation.3 | async-start | bytes 2097152 | tf_op jit(solution)/shard_map/psum | solution.py:38
  216.8 10.7 %collective-permute-start.4 = (bf16[1,16,16,512]{3,2,1,0:T(8,128)(2,1)S(1)}, bf16[1,16,16,512]{3,2,1,0:T(8,128)(2,1)S(1)}, u32[]{:S(2)}, u32[]{:S(2)}) collective-permute-start(bf16[1,16,16,512]{3,2,1,0:T(8,128)(2,1)S(1)} %get-tuple-element.378), channel_id=1, source_target_pairs={{0,1},{1,2},{2,3},{3,4},{4,5},{5,6},{6,7},{7,8},{8,9},{9,10},{10,1... | collective-permute-start | bytes 786440 | tf_op jit(solution)/shard_map/while/body/eval_jaxpr/ppermute | solution.py:27
  275.8 10.9 %collective-permute-start.4 = (bf16[1,16,16,512]{3,2,1,0:T(8,128)(2,1)S(1)}, bf16[1,16,16,512]{3,2,1,0:T(8,128)(2,1)S(1)}, u32[]{:S(2)}, u32[]{:S(2)}) collective-permute-start(bf16[1,16,16,512]{3,2,1,0:T(8,128)(2,1)S(1)} %get-tuple-element.378), channel_id=1, source_target_pairs={{0,1},{1,2},{2,3},{3,4},{4,5},{5,6},{6,7},{7,8},{8,9},{9,10},{10,1... | collective-permute-start | bytes 786440 | tf_op jit(solution)/shard_map/while/body/eval_jaxpr/ppermute | solution.py:27
  277.7 13.4 %collective-permute-start.5 = (bf16[1,16,16,512]{3,2,1,0:T(8,128)(2,1)S(1)}, bf16[1,16,16,512]{3,2,1,0:T(8,128)(2,1)S(1)}, u32[]{:S(2)}, u32[]{:S(2)}) collective-permute-start(bf16[1,16,16,512]{3,2,1,0:T(8,128)(2,1)S(1)} %get-tuple-element.378), channel_id=1, source_target_pairs={{1,0},{2,1},{3,2},{4,3},{5,4},{6,5},{7,6},{8,7},{9,8},{10,9},{11,1... | collective-permute-start | bytes 786440 | tf_op jit(solution)/shard_map/while/body/eval_jaxpr/ppermute | solution.py:29
  339.2 10.8 %collective-permute-start.4 = (bf16[1,16,16,512]{3,2,1,0:T(8,128)(2,1)S(1)}, bf16[1,16,16,512]{3,2,1,0:T(8,128)(2,1)S(1)}, u32[]{:S(2)}, u32[]{:S(2)}) collective-permute-start(bf16[1,16,16,512]{3,2,1,0:T(8,128)(2,1)S(1)} %get-tuple-element.378), channel_id=1, source_target_pairs={{0,1},{1,2},{2,3},{3,4},{4,5},{5,6},{6,7},{7,8},{8,9},{9,10},{10,1... | collective-permute-start | bytes 786440 | tf_op jit(solution)/shard_map/while/body/eval_jaxpr/ppermute | solution.py:27
  341.1 13.4 %collective-permute-start.5 = (bf16[1,16,16,512]{3,2,1,0:T(8,128)(2,1)S(1)}, bf16[1,16,16,512]{3,2,1,0:T(8,128)(2,1)S(1)}, u32[]{:S(2)}, u32[]{:S(2)}) collective-permute-start(bf16[1,16,16,512]{3,2,1,0:T(8,128)(2,1)S(1)} %get-tuple-element.378), channel_id=1, source_target_pairs={{1,0},{2,1},{3,2},{4,3},{5,4},{6,5},{7,6},{8,7},{9,8},{10,9},{11,1... | collective-permute-start | bytes 786440 | tf_op jit(solution)/shard_map/while/body/eval_jaxpr/ppermute | solution.py:29
  403.1 10.8 %collective-permute-start.4 = (bf16[1,16,16,512]{3,2,1,0:T(8,128)(2,1)S(1)}, bf16[1,16,16,512]{3,2,1,0:T(8,128)(2,1)S(1)}, u32[]{:S(2)}, u32[]{:S(2)}) collective-permute-start(bf16[1,16,16,512]{3,2,1,0:T(8,128)(2,1)S(1)} %get-tuple-element.378), channel_id=1, source_target_pairs={{0,1},{1,2},{2,3},{3,4},{4,5},{5,6},{6,7},{7,8},{8,9},{9,10},{10,1... | collective-permute-start | bytes 786440 | tf_op jit(solution)/shard_map/while/body/eval_jaxpr/ppermute | solution.py:27
  405.1 13.3 %collective-permute-start.5 = (bf16[1,16,16,512]{3,2,1,0:T(8,128)(2,1)S(1)}, bf16[1,16,16,512]{3,2,1,0:T(8,128)(2,1)S(1)}, u32[]{:S(2)}, u32[]{:S(2)}) collective-permute-start(bf16[1,16,16,512]{3,2,1,0:T(8,128)(2,1)S(1)} %get-tuple-element.378), channel_id=1, source_target_pairs={{1,0},{2,1},{3,2},{4,3},{5,4},{6,5},{7,6},{8,7},{9,8},{10,9},{11,1... | collective-permute-start | bytes 786440 | tf_op jit(solution)/shard_map/while/body/eval_jaxpr/ppermute | solution.py:29
  459.5 11.2 %collective-permute-start.4 = (bf16[1,16,16,512]{3,2,1,0:T(8,128)(2,1)S(1)}, bf16[1,16,16,512]{3,2,1,0:T(8,128)(2,1)S(1)}, u32[]{:S(2)}, u32[]{:S(2)}) collective-permute-start(bf16[1,16,16,512]{3,2,1,0:T(8,128)(2,1)S(1)} %get-tuple-element.378), channel_id=1, source_target_pairs={{0,1},{1,2},{2,3},{3,4},{4,5},{5,6},{6,7},{7,8},{8,9},{9,10},{10,1... | collective-permute-start | bytes 786440 | tf_op jit(solution)/shard_map/while/body/eval_jaxpr/ppermute | solution.py:27
  461.5 10.6 %collective-permute-start.5 = (bf16[1,16,16,512]{3,2,1,0:T(8,128)(2,1)S(1)}, bf16[1,16,16,512]{3,2,1,0:T(8,128)(2,1)S(1)}, u32[]{:S(2)}, u32[]{:S(2)}) collective-permute-start(bf16[1,16,16,512]{3,2,1,0:T(8,128)(2,1)S(1)} %get-tuple-element.378), channel_id=1, source_target_pairs={{1,0},{2,1},{3,2},{4,3},{5,4},{6,5},{7,6},{8,7},{9,8},{10,9},{11,1... | collective-permute-start | bytes 786440 | tf_op jit(solution)/shard_map/while/body/eval_jaxpr/ppermute | solution.py:29
  474.1 18.7 %collective-permute-start = (bf16[1,16,16,512]{3,2,1,0:T(8,128)(2,1)}, bf16[1,16,16,512]{3,2,1,0:T(8,128)(2,1)S(1)}, u32[]{:S(2)}, u32[]{:S(2)}) collective-permute-start(bf16[1,16,16,512]{3,2,1,0:T(8,128)(2,1)} %get-tuple-element.343), channel_id=1, source_target_pairs={{0,32},{32,64},{64,96},{96,128},{128,160},{160,192},{192,224},{1,3... | collective-permute-start | bytes 786440 | tf_op jit(solution)/shard_map/while/body/eval_jaxpr/ppermute | solution.py:12
  493.8 11.8 %collective-permute-start.1 = (bf16[1,16,16,512]{3,2,1,0:T(8,128)(2,1)S(1)}, bf16[1,16,16,512]{3,2,1,0:T(8,128)(2,1)S(1)}, u32[]{:S(2)}, u32[]{:S(2)}) collective-permute-start(bf16[1,16,16,512]{3,2,1,0:T(8,128)(2,1)S(1)} %bitcast_select_fusion.2), channel_id=1, source_target_pairs={{0,32},{32,0},{64,96},{96,64},{128,160},{160,128},{192,224},{224,1... | collective-permute-start | bytes 786440 | tf_op jit(solution)/shard_map/while/body/eval_jaxpr/ppermute | solution.py:16
  522.2 10.8 %collective-permute-start.4 = (bf16[1,16,16,512]{3,2,1,0:T(8,128)(2,1)S(1)}, bf16[1,16,16,512]{3,2,1,0:T(8,128)(2,1)S(1)}, u32[]{:S(2)}, u32[]{:S(2)}) collective-permute-start(bf16[1,16,16,512]{3,2,1,0:T(8,128)(2,1)S(1)} %get-tuple-element.378), channel_id=1, source_target_pairs={{0,1},{1,2},{2,3},{3,4},{4,5},{5,6},{6,7},{7,8},{8,9},{9,10},{10,1... | collective-permute-start | bytes 786440 | tf_op jit(solution)/shard_map/while/body/eval_jaxpr/ppermute | solution.py:27
  524.2 13.2 %collective-permute-start.5 = (bf16[1,16,16,512]{3,2,1,0:T(8,128)(2,1)S(1)}, bf16[1,16,16,512]{3,2,1,0:T(8,128)(2,1)S(1)}, u32[]{:S(2)}, u32[]{:S(2)}) collective-permute-start(bf16[1,16,16,512]{3,2,1,0:T(8,128)(2,1)S(1)} %get-tuple-element.378), channel_id=1, source_target_pairs={{1,0},{2,1},{3,2},{4,3},{5,4},{6,5},{7,6},{8,7},{9,8},{10,9},{11,1... | collective-permute-start | bytes 786440 | tf_op jit(solution)/shard_map/while/body/eval_jaxpr/ppermute | solution.py:29
  545.9 22.1 %collective-permute-start.1 = (bf16[1,16,16,512]{3,2,1,0:T(8,128)(2,1)S(1)}, bf16[1,16,16,512]{3,2,1,0:T(8,128)(2,1)S(1)}, u32[]{:S(2)}, u32[]{:S(2)}) collective-permute-start(bf16[1,16,16,512]{3,2,1,0:T(8,128)(2,1)S(1)} %bitcast_select_fusion.2), channel_id=1, source_target_pairs={{0,32},{32,0},{64,96},{96,64},{128,160},{160,128},{192,224},{224,1... | collective-permute-start | bytes 786440 | tf_op jit(solution)/shard_map/while/body/eval_jaxpr/ppermute | solution.py:16
  584.7 10.8 %collective-permute-start.4 = (bf16[1,16,16,512]{3,2,1,0:T(8,128)(2,1)S(1)}, bf16[1,16,16,512]{3,2,1,0:T(8,128)(2,1)S(1)}, u32[]{:S(2)}, u32[]{:S(2)}) collective-permute-start(bf16[1,16,16,512]{3,2,1,0:T(8,128)(2,1)S(1)} %get-tuple-element.378), channel_id=1, source_target_pairs={{0,1},{1,2},{2,3},{3,4},{4,5},{5,6},{6,7},{7,8},{8,9},{9,10},{10,1... | collective-permute-start | bytes 786440 | tf_op jit(solution)/shard_map/while/body/eval_jaxpr/ppermute | solution.py:27
  586.6 13.0 %collective-permute-start.5 = (bf16[1,16,16,512]{3,2,1,0:T(8,128)(2,1)S(1)}, bf16[1,16,16,512]{3,2,1,0:T(8,128)(2,1)S(1)}, u32[]{:S(2)}, u32[]{:S(2)}) collective-permute-start(bf16[1,16,16,512]{3,2,1,0:T(8,128)(2,1)S(1)} %get-tuple-element.378), channel_id=1, source_target_pairs={{1,0},{2,1},{3,2},{4,3},{5,4},{6,5},{7,6},{8,7},{9,8},{10,9},{11,1... | collective-permute-start | bytes 786440 | tf_op jit(solution)/shard_map/while/body/eval_jaxpr/ppermute | solution.py:29
  617.7 17.5 %collective-permute-start.2 = (bf16[1,16,16,512]{3,2,1,0:T(8,128)(2,1)S(1)}, bf16[1,16,16,512]{3,2,1,0:T(8,128)(2,1)S(1)}, u32[]{:S(2)}, u32[]{:S(2)}) collective-permute-start(bf16[1,16,16,512]{3,2,1,0:T(8,128)(2,1)S(1)} %collective-permute-done.1), channel_id=1, source_target_pairs={{0,64},{32,96},{64,0},{96,32},{128,192},{160,224},{192,128},{224,1... | collective-permute-start | bytes 786440 | tf_op jit(solution)/shard_map/while/body/eval_jaxpr/ppermute | solution.py:16
  644.7 10.8 %collective-permute-start.4 = (bf16[1,16,16,512]{3,2,1,0:T(8,128)(2,1)S(1)}, bf16[1,16,16,512]{3,2,1,0:T(8,128)(2,1)S(1)}, u32[]{:S(2)}, u32[]{:S(2)}) collective-permute-start(bf16[1,16,16,512]{3,2,1,0:T(8,128)(2,1)S(1)} %get-tuple-element.378), channel_id=1, source_target_pairs={{0,1},{1,2},{2,3},{3,4},{4,5},{5,6},{6,7},{7,8},{8,9},{9,10},{10,1... | collective-permute-start | bytes 786440 | tf_op jit(solution)/shard_map/while/body/eval_jaxpr/ppermute | solution.py:27
  646.6 13.3 %collective-permute-start.5 = (bf16[1,16,16,512]{3,2,1,0:T(8,128)(2,1)S(1)}, bf16[1,16,16,512]{3,2,1,0:T(8,128)(2,1)S(1)}, u32[]{:S(2)}, u32[]{:S(2)}) collective-permute-start(bf16[1,16,16,512]{3,2,1,0:T(8,128)(2,1)S(1)} %get-tuple-element.378), channel_id=1, source_target_pairs={{1,0},{2,1},{3,2},{4,3},{5,4},{6,5},{7,6},{8,7},{9,8},{10,9},{11,1... | collective-permute-start | bytes 786440 | tf_op jit(solution)/shard_map/while/body/eval_jaxpr/ppermute | solution.py:29
  677.5 21.2 %collective-permute-start.2 = (bf16[1,16,16,512]{3,2,1,0:T(8,128)(2,1)S(1)}, bf16[1,16,16,512]{3,2,1,0:T(8,128)(2,1)S(1)}, u32[]{:S(2)}, u32[]{:S(2)}) collective-permute-start(bf16[1,16,16,512]{3,2,1,0:T(8,128)(2,1)S(1)} %collective-permute-done.1), channel_id=1, source_target_pairs={{0,64},{32,96},{64,0},{96,32},{128,192},{160,224},{192,128},{224,1... | collective-permute-start | bytes 786440 | tf_op jit(solution)/shard_map/while/body/eval_jaxpr/ppermute | solution.py:16
  707.1 11.1 %collective-permute-start.4 = (bf16[1,16,16,512]{3,2,1,0:T(8,128)(2,1)S(1)}, bf16[1,16,16,512]{3,2,1,0:T(8,128)(2,1)S(1)}, u32[]{:S(2)}, u32[]{:S(2)}) collective-permute-start(bf16[1,16,16,512]{3,2,1,0:T(8,128)(2,1)S(1)} %get-tuple-element.378), channel_id=1, source_target_pairs={{0,1},{1,2},{2,3},{3,4},{4,5},{5,6},{6,7},{7,8},{8,9},{9,10},{10,1... | collective-permute-start | bytes 786440 | tf_op jit(solution)/shard_map/while/body/eval_jaxpr/ppermute | solution.py:27
  709.0 13.3 %collective-permute-start.5 = (bf16[1,16,16,512]{3,2,1,0:T(8,128)(2,1)S(1)}, bf16[1,16,16,512]{3,2,1,0:T(8,128)(2,1)S(1)}, u32[]{:S(2)}, u32[]{:S(2)}) collective-permute-start(bf16[1,16,16,512]{3,2,1,0:T(8,128)(2,1)S(1)} %get-tuple-element.378), channel_id=1, source_target_pairs={{1,0},{2,1},{3,2},{4,3},{5,4},{6,5},{7,6},{8,7},{9,8},{10,9},{11,1... | collective-permute-start | bytes 786440 | tf_op jit(solution)/shard_map/while/body/eval_jaxpr/ppermute | solution.py:29
  748.4 19.4 %collective-permute-start.3 = (bf16[1,16,16,512]{3,2,1,0:T(8,128)(2,1)S(1)}, bf16[1,16,16,512]{3,2,1,0:T(8,128)(2,1)S(1)}, u32[]{:S(2)}, u32[]{:S(2)}) collective-permute-start(bf16[1,16,16,512]{3,2,1,0:T(8,128)(2,1)S(1)} %collective-permute-done.2), channel_id=1, source_target_pairs={{0,128},{32,160},{64,192},{96,224},{128,0},{160,32},{192,64},{224,... | collective-permute-start | bytes 786440 | tf_op jit(solution)/shard_map/while/body/eval_jaxpr/ppermute | solution.py:16
  768.3 12.6 %collective-permute-start.4 = (bf16[1,16,16,512]{3,2,1,0:T(8,128)(2,1)S(1)}, bf16[1,16,16,512]{3,2,1,0:T(8,128)(2,1)S(1)}, u32[]{:S(2)}, u32[]{:S(2)}) collective-permute-start(bf16[1,16,16,512]{3,2,1,0:T(8,128)(2,1)S(1)} %get-tuple-element.378), channel_id=1, source_target_pairs={{0,1},{1,2},{2,3},{3,4},{4,5},{5,6},{6,7},{7,8},{8,9},{9,10},{10,1... | collective-permute-start | bytes 786440 | tf_op jit(solution)/shard_map/while/body/eval_jaxpr/ppermute | solution.py:27
  770.3 13.1 %collective-permute-start.5 = (bf16[1,16,16,512]{3,2,1,0:T(8,128)(2,1)S(1)}, bf16[1,16,16,512]{3,2,1,0:T(8,128)(2,1)S(1)}, u32[]{:S(2)}, u32[]{:S(2)}) collective-permute-start(bf16[1,16,16,512]{3,2,1,0:T(8,128)(2,1)S(1)} %get-tuple-element.378), channel_id=1, source_target_pairs={{1,0},{2,1},{3,2},{4,3},{5,4},{6,5},{7,6},{8,7},{9,8},{10,9},{11,1... | collective-permute-start | bytes 786440 | tf_op jit(solution)/shard_map/while/body/eval_jaxpr/ppermute | solution.py:29
  807.4 23.1 %collective-permute-start.3 = (bf16[1,16,16,512]{3,2,1,0:T(8,128)(2,1)S(1)}, bf16[1,16,16,512]{3,2,1,0:T(8,128)(2,1)S(1)}, u32[]{:S(2)}, u32[]{:S(2)}) collective-permute-start(bf16[1,16,16,512]{3,2,1,0:T(8,128)(2,1)S(1)} %collective-permute-done.2), channel_id=1, source_target_pairs={{0,128},{32,160},{64,192},{96,224},{128,0},{160,32},{192,64},{224,... | collective-permute-start | bytes 786440 | tf_op jit(solution)/shard_map/while/body/eval_jaxpr/ppermute | solution.py:16
  831.1 10.8 %collective-permute-start.4 = (bf16[1,16,16,512]{3,2,1,0:T(8,128)(2,1)S(1)}, bf16[1,16,16,512]{3,2,1,0:T(8,128)(2,1)S(1)}, u32[]{:S(2)}, u32[]{:S(2)}) collective-permute-start(bf16[1,16,16,512]{3,2,1,0:T(8,128)(2,1)S(1)} %get-tuple-element.378), channel_id=1, source_target_pairs={{0,1},{1,2},{2,3},{3,4},{4,5},{5,6},{6,7},{7,8},{8,9},{9,10},{10,1... | collective-permute-start | bytes 786440 | tf_op jit(solution)/shard_map/while/body/eval_jaxpr/ppermute | solution.py:27
  833.0 13.1 %collective-permute-start.5 = (bf16[1,16,16,512]{3,2,1,0:T(8,128)(2,1)S(1)}, bf16[1,16,16,512]{3,2,1,0:T(8,128)(2,1)S(1)}, u32[]{:S(2)}, u32[]{:S(2)}) collective-permute-start(bf16[1,16,16,512]{3,2,1,0:T(8,128)(2,1)S(1)} %get-tuple-element.378), channel_id=1, source_target_pairs={{1,0},{2,1},{3,2},{4,3},{5,4},{6,5},{7,6},{8,7},{9,8},{10,9},{11,1... | collective-permute-start | bytes 786440 | tf_op jit(solution)/shard_map/while/body/eval_jaxpr/ppermute | solution.py:29
  (50 other events, 331.9 us)
Sparse Core Ops, SparseCore 0:
  10.0 79.8 all-gather.4
  92.6 82.7 all-gather.2
  849.3 95.1 all-reduce.3
